TPU v7x, 32 devices: a whole 2x2x4 slice. The times are simulated.
32 devices in a mesh: section: 2 (over core), seq: 16 (over z, y, x).
Axes of the slice: x: 2, y: 2, z: 4, core: 2. Of those that a mesh axis runs over, the one named last changes fastest.
Arguments:
- tokens: bfloat16 [1, 2048, 1024], P(None, 'seq'), may hold values from -24 to 24
- neighbor_ids: int32 [16, 9], P('seq'), may hold values from 0 to 15, as said below
- neighbor_count: int32 [16], P('seq'), may hold values from 1 to 9, as said below
- w_query: bfloat16 [2, 1024, 1024], P('section')
- w_key: bfloat16 [2, 1024, 1024], P('section')
- w_value: bfloat16 [2, 1024, 1024], P('section'), may hold values from -0.1875 to 0.1875
- w_out: bfloat16 [2, 1024, 1024], P('section'), may hold values from -0.1875 to 0.1875
- norm_gain: float32 [2, 1024], P('section'), may hold values from 0.5 to 3
- w_up: bfloat16 [2, 4096, 1024], P('section', 'seq'), may hold values from -0.1875 to 0.1875
- w_down: bfloat16 [2, 4096, 1024], P('section', 'seq'), may hold values from -0.09375 to 0.09375
- mlp_gain: float32 [2, 1024], P('section'), may hold values from 0.5 to 2
Outputs:
- layer_outputs: bfloat16 [2, 1, 2048, 1024], P('section', None, 'seq')
Inputs may be any that keep to these rules, and one draw needn't show every extreme that they name: `neighbor_ids`: blocks lie row by row on a map 4 blocks wide. Row b lists in its first neighbor_count[b] entries distinct blocks among b and the up to eight blocks beside it on the map (diagonals included), b first; its other entries equal b. `neighbor_count`: some block has 9.
All inputs are finite; a program needn't handle non-finite values.
Results may differ from a plain program's by a relative error of at most 0.017.
Values may be sent and summed in bfloat16 or wider, within the bound.
A program may use at most 128 MiB of HBM per device.

v0:
```python
import math

import jax
import jax.numpy as jnp
from jax import lax
from jax.sharding import PartitionSpec as P

HEADS = 16
BLK = 128
ROW = 4


def from_behind(block, axis, distance):
    devices = range(lax.axis_size(axis))
    route = [(i - distance, i) for i in devices if i - distance in devices]
    return lax.ppermute(block, axis, route)


def fetch_band(packed, reach_count):
    blocks_here = packed.shape[0]
    distances = [0, 1, -1, ROW - 1, 1 - ROW, ROW, -ROW, ROW + 1, -ROW - 1]
    wanted = set(
        (
            (position + jump_size) // blocks_here
            for position in range(blocks_here)
            for jump_size in distances
        )
    )
    pieces = []
    for offset in range(-reach_count, reach_count + 1):
        if offset == 0:
            pieces.append(packed)
        elif offset in wanted:
            pieces.append(from_behind(packed, "seq", -offset))
        else:
            pieces.append(jnp.zeros_like(packed))
    return jnp.concatenate(pieces, axis=0)


def soft_weights(scores, live, score_scale):
    scaled = jnp.where(live, scores * score_scale, -jnp.inf)
    row_max = jnp.max(scaled, axis=-1, keepdims=True)
    exponent = jnp.exp(scaled - row_max)
    return (exponent / jnp.sum(exponent, axis=-1, keepdims=True)).astype(jnp.bfloat16)


def rms_normed(widened, gain):
    return (
        widened * lax.rsqrt(jnp.mean(widened * widened, axis=-1, keepdims=True) + 1e-05) * gain
    ).astype(jnp.bfloat16)


def prepare(inputs, gain, query_weight, key_weight, value_weight):
    tok_rows, width = inputs.shape
    normed = rms_normed(inputs.astype(jnp.float32), gain)
    queries = jnp.dot(normed, query_weight, preferred_element_type=jnp.float32).astype(jnp.bfloat16)
    keys = jnp.dot(normed, key_weight, preferred_element_type=jnp.float32).astype(jnp.bfloat16)
    values = jnp.dot(normed, value_weight, preferred_element_type=jnp.float32).astype(jnp.bfloat16)
    packed = jnp.concatenate([keys, values], axis=-1).reshape(tok_rows // BLK, BLK, 2 * width)
    return (queries, packed)


def finish(
    inputs,
    queries,
    band_rows,
    neighbor_ids,
    neighbor_count,
    out_weight,
    up_weight,
    down_weight,
    second_gain,
    device,
    reach_count,
):
    tok_rows, width = inputs.shape
    blocks_here = tok_rows // BLK
    slot_total = neighbor_ids.shape[1]
    head_size = width // HEADS
    score_scale = 1.0 / math.sqrt(head_size)
    band_start = (device - reach_count) * blocks_here
    slot_live = jnp.arange(slot_total, dtype=jnp.int32)[None, :] < neighbor_count[:, None]
    query_blocks = queries.reshape(blocks_here, BLK, HEADS, head_size)
    band_keys = band_rows[..., :width]
    band_values = band_rows[..., width:]
    local_ids = neighbor_ids - band_start
    key_set = jnp.take(band_keys, local_ids, axis=0).reshape(
        blocks_here, slot_total * BLK, HEADS, head_size
    )
    value_set = jnp.take(band_values, local_ids, axis=0).reshape(
        blocks_here, slot_total * BLK, HEADS, head_size
    )
    key_live = jnp.repeat(slot_live, BLK, axis=1)
    scores = jnp.einsum(
        "bqhd,bkhd->bhqk", query_blocks, key_set, preferred_element_type=jnp.float32
    )
    probs = soft_weights(scores, key_live[:, None, None, :], score_scale)
    mixed = jnp.einsum(
        "bhqk,bkhd->bqhd", probs, value_set, preferred_element_type=jnp.float32
    ).astype(jnp.bfloat16)
    mixed = mixed.reshape(tok_rows, width)
    attended = (
        inputs.astype(jnp.float32) + jnp.dot(mixed, out_weight, preferred_element_type=jnp.float32)
    ).astype(jnp.bfloat16)
    attended_wide = attended.astype(jnp.float32)
    second = rms_normed(attended_wide, second_gain)
    upper_rows = lax.dot_general(
        second, up_weight, (((1,), (1,)), ((), ())), preferred_element_type=jnp.float32
    )
    hidden = jax.nn.gelu(upper_rows, approximate=True).astype(jnp.bfloat16)
    return (
        attended_wide + jnp.dot(hidden, down_weight, preferred_element_type=jnp.float32)
    ).astype(jnp.bfloat16)


def local(
    tokens,
    neighbor_ids,
    neighbor_count,
    w_query,
    w_key,
    w_value,
    w_out,
    norm_gain,
    w_up,
    w_down,
    mlp_gain,
):
    graphs, tok_rows, width = tokens.shape
    blocks_here = tok_rows // BLK
    reach_count = (ROW + blocks_here) // blocks_here
    sections = lax.axis_size("section")
    section_index = lax.axis_index("section")
    device = lax.axis_index("seq")
    ticks = graphs + sections - 1
    up_whole, down_whole = (
        lax.all_gather(w_up, "seq", axis=1, tiled=True),
        lax.all_gather(w_down, "seq", axis=1, tiled=True),
    )
    results = jnp.zeros((1, graphs, tok_rows, width), jnp.bfloat16)
    incoming = jnp.zeros((tok_rows, width), jnp.bfloat16)
    for tick_index in range(ticks):
        first_input = tokens[min(tick_index, graphs - 1)]
        layer_input = jnp.where(section_index == 0, first_input, incoming)
        graph_index = tick_index - section_index
        active = (graph_index >= 0) & (graph_index < graphs)

        def run_prepare(operand_rows):
            return prepare(operand_rows, norm_gain[0], w_query[0], w_key[0], w_value[0])

        def skip_prepare(operand_rows):
            return (
                jnp.zeros((tok_rows, width), jnp.bfloat16),
                jnp.zeros((blocks_here, BLK, 2 * width), jnp.bfloat16),
            )

        queries, packed = lax.cond(active, run_prepare, skip_prepare, layer_input)
        band_rows = fetch_band(packed, reach_count)

        def run_finish(operand_set):
            return finish(
                operand_set[0],
                operand_set[1],
                operand_set[2],
                neighbor_ids,
                neighbor_count,
                w_out[0],
                up_whole[0],
                down_whole[0],
                mlp_gain[0],
                device,
                reach_count,
            )

        def skip_finish(operand_set):
            return jnp.zeros((tok_rows, width), jnp.bfloat16)

        layer_output = lax.cond(active, run_finish, skip_finish, (layer_input, queries, band_rows))
        results = results.at[0, 0].set(jnp.where(graph_index == 0, layer_output, results[0, 0]))
        if tick_index + 1 < ticks:
            incoming = from_behind(layer_output, "section", 1)
    return results


def solution(mesh):
    in_specs = (
        P(None, "seq", None),
        P("seq", None),
        P("seq"),
        P("section", None, None),
        P("section", None, None),
        P("section", None, None),
        P("section", None, None),
        P("section", None),
        P("section", "seq", None),
        P("section", "seq", None),
        P("section", None),
    )
    out_specs = P("section", None, "seq", None)
    return jax.shard_map(local, mesh=mesh, in_specs=in_specs, out_specs=out_specs, check_vma=False)
```

profile of v0, /device:TPU:13, one launch (start us, length us, event | category | flops | bytes accessed | tf_op | source)
XLA Modules:
  0.0 487.6 jit_solution(1373884698683510926)
XLA Ops:
  9.1 4.1 collective-permute-start
  29.3 10.8 %collective-permute-done.1 = bf16[1,128,2048]{2,1,0:T(8,128)(2,1)} collective-permute-done((bf16[1,128,2048]{2,1,0:T(8,128)(2,1)S(1)}, bf16[1,128,2048]{2,1,0:T(8,128)(2,1)}, u32[]{:S(2)}, u32[]{:S(2)}) %collective-permute-start.1) | collective-permute-done | bytes 524320 | tf_op jit(solution)/shard_map/ppermute | solution.py:16
  43.9 10.5 %collective-permute-done.2 = bf16[1,128,2048]{2,1,0:T(8,128)(2,1)} collective-permute-done((bf16[1,128,2048]{2,1,0:T(8,128)(2,1)S(1)}, bf16[1,128,2048]{2,1,0:T(8,128)(2,1)}, u32[]{:S(2)}, u32[]{:S(2)}) %collective-permute-start.2) | collective-permute-done | bytes 524320 | tf_op jit(solution)/shard_map/ppermute | solution.py:16
  60.7 14.5 %collective-permute-done.4 = bf16[1,128,2048]{2,1,0:T(8,128)(2,1)S(1)} collective-permute-done((bf16[1,128,2048]{2,1,0:T(8,128)(2,1)S(1)}, bf16[1,128,2048]{2,1,0:T(8,128)(2,1)S(1)}, u32[]{:S(2)}, u32[]{:S(2)}) %collective-permute-start.4) | collective-permute-done | bytes 524320 | tf_op jit(solution)/shard_map/ppermute | solution.py:16
  77.8 11.1 %collective-permute-done.6 = bf16[1,128,2048]{2,1,0:T(8,128)(2,1)S(1)} collective-permute-done((bf16[1,128,2048]{2,1,0:T(8,128)(2,1)S(1)}, bf16[1,128,2048]{2,1,0:T(8,128)(2,1)S(1)}, u32[]{:S(2)}, u32[]{:S(2)}) %collective-permute-start.6) | collective-permute-done | bytes 524320 | tf_op jit(solution)/shard_map/ppermute | solution.py:16
  89.7 9.5 %collective-permute-done.7 = bf16[1,128,2048]{2,1,0:T(8,128)(2,1)S(1)} collective-permute-done((bf16[1,128,2048]{2,1,0:T(8,128)(2,1)S(1)}, bf16[1,128,2048]{2,1,0:T(8,128)(2,1)S(1)}, u32[]{:S(2)}, u32[]{:S(2)}) %collective-permute-start.7) | collective-permute-done | bytes 524320 | tf_op jit(solution)/shard_map/ppermute | solution.py:16
  100.1 67.6 %all-gather.3.cloned.1.call-done = bf16[1,4096,1024]{2,1,0:T(8,128)(2,1)} async-done(((bf16[1,256,1024]{2,1,0:T(8,128)(2,1)}), bf16[1,4096,1024]{2,1,0:T(8,128)(2,1)}) %all-gather.3.cloned.1.call-update) | async-done | bytes 8388624 | tf_op jit(solution)/shard_map/all_gather | solution.py:137
  167.7 113.8 %all-gather.5.cloned.1.call-done = bf16[1,4096,1024]{2,1,0:T(8,128)(2,1)} async-done(((bf16[1,256,1024]{2,1,0:T(8,128)(2,1)}), bf16[1,4096,1024]{2,1,0:T(8,128)(2,1)}) %all-gather.5.cloned.1.call-update) | async-done | bytes 8388624 | tf_op jit(solution)/shard_map/all_gather | solution.py:138
  283.1 60.4 %collective-permute-done.8 = bf16[128,1024]{1,0:T(8,128)(2,1)S(1)} collective-permute-done((bf16[128,1024]{1,0:T(8,128)(2,1)S(1)}, bf16[128,1024]{1,0:T(8,128)(2,1)S(1)}, u32[]{:S(2)}, u32[]{:S(2)}) %collective-permute-start.8) | collective-permute-done | bytes 262176 | tf_op jit(solution)/shard_map/ppermute | solution.py:16
  344.5 5.0 %conditional.6 = (bf16[128,1024]{1,0:T(8,128)(2,1)S(1)}, bf16[1,128,2048]{2,1,0:T(8,128)(2,1)S(1)}) conditional(s32[]{:T(128)} %convert_element_type.100, () %tuple.47, (bf16[128,1024]{1,0:T(8,128)(2,1)S(1)}, f32[1,1024]{1,0:T(1,128)S(1)}, bf16[1,1024,1024]{2,1,0:T(8,128)(2,1)}, bf16[1,1024,1024]{2,1,0:T(8,128)(2,1)}, ...), branch_computations={%region_8.10_spmd, %region_9.12_spmd} | conditional | flops 808714368 | bytes 17579052 | solution.py:157
  360.7 4.3 collective-permute-start.13
  369.7 7.0 %collective-permute-done.10 = bf16[1,128,2048]{2,1,0:T(8,128)(2,1)S(1)} collective-permute-done((bf16[1,128,2048]{2,1,0:T(8,128)(2,1)S(1)}, bf16[1,128,2048]{2,1,0:T(8,128)(2,1)S(1)}, u32[]{:S(2)}, u32[]{:S(2)}) %collective-permute-start.10) | collective-permute-done | bytes 524320 | tf_op jit(solution)/shard_map/ppermute | solution.py:16
  379.5 10.6 %collective-permute-done.11 = bf16[1,128,2048]{2,1,0:T(8,128)(2,1)S(1)} collective-permute-done((bf16[1,128,2048]{2,1,0:T(8,128)(2,1)S(1)}, bf16[1,128,2048]{2,1,0:T(8,128)(2,1)S(1)}, u32[]{:S(2)}, u32[]{:S(2)}) %collective-permute-start.11) | collective-permute-done | bytes 524320 | tf_op jit(solution)/shard_map/ppermute | solution.py:16
  393.6 17.1 %collective-permute-done.12 = bf16[1,128,2048]{2,1,0:T(8,128)(2,1)S(1)} collective-permute-done((bf16[1,128,2048]{2,1,0:T(8,128)(2,1)S(1)}, bf16[1,128,2048]{2,1,0:T(8,128)(2,1)S(1)}, u32[]{:S(2)}, u32[]{:S(2)}) %collective-permute-start.12) | collective-permute-done | bytes 524320 | tf_op jit(solution)/shard_map/ppermute | solution.py:16
  412.5 4.5 collective-permute-done.13
  421.2 58.7 %conditional.7 = (bf16[128,1024]{1,0:T(8,128)(2,1)S(1)}) conditional(s32[]{:T(128)} %convert_element_type.100, () %tuple.42, (bf16[128,1024]{1,0:T(8,128)(2,1)S(1)}, bf16[11,128,2048]{2,1,0:T(8,128)(2,1)}, s32[]{:T(128)}, s32[1,9]{1,0:T(1,128)S(1)}, s32[1]{0:T(128)}, /*index=5*/bf16[128,1024]{1,0:T(8,128)(2,1)S(1)}, ...), branch_computations={%region_11.13_spmd, %region_12.17_spmd} | conditional | flops 3047426304 | bytes 114586176 | solution.py:178
  421.9 5.2 %fusion.164 = (bf16[11,128,1024]{2,1,0:T(8,128)(2,1)}, bf16[11,128,1024]{2,1,0:T(8,128)(2,1)S(1)}) fusion(bf16[11,128,2048]{2,1,0:T(8,128)(2,1)} %get-tuple-element.117), kind=kLoop, calls=%fused_computation.169 | loop fusion | bytes 11534336 | tf_op jit(solution)/shard_map/cond/branch_1_fun/slice | solution.py:85
  427.1 4.1 gather_fusion.2
  433.6 4.3 bitcast_select_fusion.3
  437.9 7.3 %reshape.288 = bf16[1152,16,64]{2,1,0:T(8,128)(2,1)} reshape(bf16[1,9,128,1024]{3,2,1,0:T(8,128)(2,1)} %get-tuple-element.189) | data formatting | bytes 4718592 | tf_op jit(solution)/shard_map/reshape.89
  449.4 6.7 %fusion.165 = (f32[16,128]{1,0:T(8,128)S(1)}, f32[16,128,1152]{1,2,0:T(8,128)}) fusion(f32[16,1152,128]{2,1,0:T(8,128)S(1)} %fusion.111, pred[1152]{0:T(1024)(128)(4,1)S(1)} %broadcast_bitcast_fusion.1), kind=kOutput, calls=%fused_computation.170 | output fusion | flops 14156927 | bytes 18883712 | tf_op jit(solution)/shard_map/cond/branch_1_fun/sub | solution.py:43
  456.1 4.7 reshape.287
  460.8 8.2 %fusion.141 = bf16[16,64,128]{2,1,0:T(8,128)(2,1)S(1)} fusion(f32[16,128,1152]{1,2,0:T(8,128)} %get-tuple-element.191, f32[16,128]{1,0:T(8,128)S(1)} %get-tuple-element.190, bf16[1152,16,64]{2,1,0:T(8,128)(2,1)} %reshape.287), kind=kOutput, calls=%fused_computation.123 | convolution fusion | flops 306839552 | bytes 12066816 | tf_op jit(solution)/shard_map/cond/branch_1_fun/bhqk,bkhd->bqhd/dot_general | solution.py:98
  469.6 10.0 %fusion.138 = bf16[128,1024]{1,0:T(8,128)(2,1)S(1)} fusion(f32[128,1024]{1,0:T(8,128)S(1)} %get-tuple-element.193, bf16[1,4096,1024]{2,1,0:T(8,128)(2,1)} %get-tuple-element.125, bf16[1,4096,1024]{2,1,0:T(8,128)(2,1)} %get-tuple-element.124, f32[1024]{0:T(1024)S(1)} %bitcast.180, f32[128]{0:T(128)S(1)} %add_rsqrt_fusion.3), kind=kOutput, calls=%fused_computation.122 | convolution fusion | flops 2152857600 | bytes 17568256 | tf_op jit(solution)/shard_map/cond/branch_1_fun/dot_general | solution.py:112
  (89 shorter events, 77.1 us)
Async XLA Ops:
  6.5 161.2 %all-gather.3.cloned.1.call-start = ((), (), s32[]{:S(2)}) async-start(), calls=%async_computation | async-start | bytes 8912896 | tf_op jit(solution)/shard_map/all_gather | solution.py:137
  7.3 274.3 %all-gather.5.cloned.1.call-start = ((), (), s32[]{:S(2)}) async-start(), calls=%async_computation.1 | async-start | bytes 8912896 | tf_op jit(solution)/shard_map/all_gather | solution.py:138
  9.1 16.4 %collective-permute-start = (bf16[1,128,2048]{2,1,0:T(8,128)(2,1)S(1)}, bf16[1,128,2048]{2,1,0:T(8,128)(2,1)S(1)}, u32[]{:S(2)}, u32[]{:S(2)}) collective-permute-start(bf16[1,128,2048]{2,1,0:T(8,128)(2,1)S(1)} %get-tuple-element.130), channel_id=1, source_target_pairs={{0,5},{1,6},{2,7},{3,8},{4,9},{5,10},{6,11},{7,12},{8,13},{9,14},{... | collective-permute-start | bytes 1572872 | tf_op jit(solution)/shard_map/ppermute | solution.py:16
  13.2 26.8 %collective-permute-start.1 = (bf16[1,128,2048]{2,1,0:T(8,128)(2,1)S(1)}, bf16[1,128,2048]{2,1,0:T(8,128)(2,1)}, u32[]{:S(2)}, u32[]{:S(2)}) collective-permute-start(bf16[1,128,2048]{2,1,0:T(8,128)(2,1)S(1)} %get-tuple-element.130), channel_id=1, source_target_pairs={{0,4},{1,5},{2,6},{3,7},{4,8},{5,9},{6,10},{7,11},{8,12},{9,13},{1... | collective-permute-start | bytes 1572872 | tf_op jit(solution)/shard_map/ppermute | solution.py:16
  16.5 37.9 %collective-permute-start.2 = (bf16[1,128,2048]{2,1,0:T(8,128)(2,1)S(1)}, bf16[1,128,2048]{2,1,0:T(8,128)(2,1)}, u32[]{:S(2)}, u32[]{:S(2)}) collective-permute-start(bf16[1,128,2048]{2,1,0:T(8,128)(2,1)S(1)} %get-tuple-element.130), channel_id=1, source_target_pairs={{0,3},{1,4},{2,5},{3,6},{4,7},{5,8},{6,9},{7,10},{8,11},{9,12},{10... | collective-permute-start | bytes 1572872 | tf_op jit(solution)/shard_map/ppermute | solution.py:16
  19.3 39.8 %collective-permute-start.3 = (bf16[1,128,2048]{2,1,0:T(8,128)(2,1)S(1)}, bf16[1,128,2048]{2,1,0:T(8,128)(2,1)S(1)}, u32[]{:S(2)}, u32[]{:S(2)}) collective-permute-start(bf16[1,128,2048]{2,1,0:T(8,128)(2,1)S(1)} %get-tuple-element.130), channel_id=1, source_target_pairs={{0,1},{1,2},{2,3},{3,4},{4,5},{5,6},{6,7},{7,8},{8,9},{9,10},{10,1... | collective-permute-start | bytes 1572872 | tf_op jit(solution)/shard_map/ppermute | solution.py:16
  21.5 53.8 %collective-permute-start.4 = (bf16[1,128,2048]{2,1,0:T(8,128)(2,1)S(1)}, bf16[1,128,2048]{2,1,0:T(8,128)(2,1)S(1)}, u32[]{:S(2)}, u32[]{:S(2)}) collective-permute-start(bf16[1,128,2048]{2,1,0:T(8,128)(2,1)S(1)} %get-tuple-element.130), channel_id=1, source_target_pairs={{1,0},{2,1},{3,2},{4,3},{5,4},{6,5},{7,6},{8,7},{9,8},{10,9},{11,1... | collective-permute-start | bytes 1572872 | tf_op jit(solution)/shard_map/ppermute | solution.py:16
  25.5 51.5 %collective-permute-start.5 = (bf16[1,128,2048]{2,1,0:T(8,128)(2,1)S(1)}, bf16[1,128,2048]{2,1,0:T(8,128)(2,1)S(1)}, u32[]{:S(2)}, u32[]{:S(2)}) collective-permute-start(bf16[1,128,2048]{2,1,0:T(8,128)(2,1)S(1)} %get-tuple-element.130), channel_id=1, source_target_pairs={{3,0},{4,1},{5,2},{6,3},{7,4},{8,5},{9,6},{10,7},{11,8},{12,9},{13... | collective-permute-start | bytes 1572872 | tf_op jit(solution)/shard_map/ppermute | solution.py:16
  29.3 252.3 %copy-start.10 = (s32[1,9]{1,0:T(1,128)S(1)}, s32[1,9]{1,0:T(1,128)}, u32[]{:S(2)}) copy-start(s32[1,9]{1,0:T(1,128)} %param.26) | copy-start | bytes 112
  29.3 252.3 %copy-start.11 = (f32[1,1024]{1,0:T(1,128)S(1)}, f32[1,1024]{1,0:T(1,128)}, u32[]{:S(2)}) copy-start(f32[1,1024]{1,0:T(1,128)} %param.35) | copy-start | bytes 12292
  40.1 48.8 %collective-permute-start.6 = (bf16[1,128,2048]{2,1,0:T(8,128)(2,1)S(1)}, bf16[1,128,2048]{2,1,0:T(8,128)(2,1)S(1)}, u32[]{:S(2)}, u32[]{:S(2)}) collective-permute-start(bf16[1,128,2048]{2,1,0:T(8,128)(2,1)S(1)} %get-tuple-element.130), channel_id=1, source_target_pairs={{4,0},{5,1},{6,2},{7,3},{8,4},{9,5},{10,6},{11,7},{12,8},{13,9},{1... | collective-permute-start | bytes 1572872 | tf_op jit(solution)/shard_map/ppermute | solution.py:16
  54.4 44.9 %collective-permute-start.7 = (bf16[1,128,2048]{2,1,0:T(8,128)(2,1)S(1)}, bf16[1,128,2048]{2,1,0:T(8,128)(2,1)S(1)}, u32[]{:S(2)}, u32[]{:S(2)}) collective-permute-start(bf16[1,128,2048]{2,1,0:T(8,128)(2,1)S(1)} %get-tuple-element.130), channel_id=1, source_target_pairs={{5,0},{6,1},{7,2},{8,3},{9,4},{10,5},{11,6},{12,7},{13,8},{14,9},{... | collective-permute-start | bytes 1572872 | tf_op jit(solution)/shard_map/ppermute | solution.py:16
  281.5 62.9 %copy-start.8 = (f32[1,1024]{1,0:T(1,128)S(1)}, f32[1,1024]{1,0:T(1,128)}, u32[]{:S(2)}) copy-start(f32[1,1024]{1,0:T(1,128)} %param.32) | copy-start | bytes 12292
  281.8 62.7 %copy-start.4 = (bf16[128,1024]{1,0:T(8,128)(2,1)}, bf16[128,1024]{1,0:T(8,128)(2,1)S(1)}, u32[]{:S(2)}) copy-start(bf16[128,1024]{1,0:T(8,128)(2,1)S(1)} %get-tuple-element.202) | copy-start | bytes 786436
  281.8 61.7 %collective-permute-start.8 = (bf16[128,1024]{1,0:T(8,128)(2,1)S(1)}, bf16[128,1024]{1,0:T(8,128)(2,1)S(1)}, u32[]{:S(2)}, u32[]{:S(2)}) collective-permute-start(bf16[128,1024]{1,0:T(8,128)(2,1)S(1)} %get-tuple-element.202), channel_id=1, source_target_pairs={{0,16},{1,17},{2,18},{3,19},{4,20},{5,21},{6,22},{7,23},{8,24},{9,... | collective-permute-start | bytes 786440 | tf_op jit(solution)/shard_map/ppermute | solution.py:16
  349.5 17.4 %collective-permute-start.9 = (bf16[1,128,2048]{2,1,0:T(8,128)(2,1)S(1)}, bf16[1,128,2048]{2,1,0:T(8,128)(2,1)S(1)}, u32[]{:S(2)}, u32[]{:S(2)}) collective-permute-start(bf16[1,128,2048]{2,1,0:T(8,128)(2,1)S(1)} %get-tuple-element.132), channel_id=1, source_target_pairs={{0,5},{1,6},{2,7},{3,8},{4,9},{5,10},{6,11},{7,12},{8,13},{9,14},{... | collective-permute-start | bytes 1572872 | tf_op jit(solution)/shard_map/ppermute | solution.py:16
  352.9 23.7 %collective-permute-start.10 = (bf16[1,128,2048]{2,1,0:T(8,128)(2,1)S(1)}, bf16[1,128,2048]{2,1,0:T(8,128)(2,1)S(1)}, u32[]{:S(2)}, u32[]{:S(2)}) collective-permute-start(bf16[1,128,2048]{2,1,0:T(8,128)(2,1)S(1)} %get-tuple-element.132), channel_id=1, source_target_pairs={{0,4},{1,5},{2,6},{3,7},{4,8},{5,9},{6,10},{7,11},{8,12},{9,13},{1... | collective-permute-start | bytes 1572872 | tf_op jit(solution)/shard_map/ppermute | solution.py:16
  355.1 35.0 %collective-permute-start.11 = (bf16[1,128,2048]{2,1,0:T(8,128)(2,1)S(1)}, bf16[1,128,2048]{2,1,0:T(8,128)(2,1)S(1)}, u32[]{:S(2)}, u32[]{:S(2)}) collective-permute-start(bf16[1,128,2048]{2,1,0:T(8,128)(2,1)S(1)} %get-tuple-element.132), channel_id=1, source_target_pairs={{0,3},{1,4},{2,5},{3,6},{4,7},{5,8},{6,9},{7,10},{8,11},{9,12},{10... | collective-permute-start | bytes 1572872 | tf_op jit(solution)/shard_map/ppermute | solution.py:16
  358.8 52.0 %collective-permute-start.12 = (bf16[1,128,2048]{2,1,0:T(8,128)(2,1)S(1)}, bf16[1,128,2048]{2,1,0:T(8,128)(2,1)S(1)}, u32[]{:S(2)}, u32[]{:S(2)}) collective-permute-start(bf16[1,128,2048]{2,1,0:T(8,128)(2,1)S(1)} %get-tuple-element.132), channel_id=1, source_target_pairs={{0,1},{1,2},{2,3},{3,4},{4,5},{5,6},{6,7},{7,8},{8,9},{9,10},{10,1... | collective-permute-start | bytes 1572872 | tf_op jit(solution)/shard_map/ppermute | solution.py:16
  360.7 56.2 %collective-permute-start.13 = (bf16[1,128,2048]{2,1,0:T(8,128)(2,1)S(1)}, bf16[1,128,2048]{2,1,0:T(8,128)(2,1)S(1)}, u32[]{:S(2)}, u32[]{:S(2)}) collective-permute-start(bf16[1,128,2048]{2,1,0:T(8,128)(2,1)S(1)} %get-tuple-element.132), channel_id=1, source_target_pairs={{1,0},{2,1},{3,2},{4,3},{5,4},{6,5},{7,6},{8,7},{9,8},{10,9},{11,1... | collective-permute-start | bytes 1572872 | tf_op jit(solution)/shard_map/ppermute | solution.py:16
  366.9 51.8 %collective-permute-start.14 = (bf16[1,128,2048]{2,1,0:T(8,128)(2,1)S(1)}, bf16[1,128,2048]{2,1,0:T(8,128)(2,1)S(1)}, u32[]{:S(2)}, u32[]{:S(2)}) collective-permute-start(bf16[1,128,2048]{2,1,0:T(8,128)(2,1)S(1)} %get-tuple-element.132), channel_id=1, source_target_pairs={{3,0},{4,1},{5,2},{6,3},{7,4},{8,5},{9,6},{10,7},{11,8},{12,9},{13... | collective-permute-start | bytes 1572872 | tf_op jit(solution)/shard_map/ppermute | solution.py:16
  376.7 42.9 %collective-permute-start.15 = (bf16[1,128,2048]{2,1,0:T(8,128)(2,1)S(1)}, bf16[1,128,2048]{2,1,0:T(8,128)(2,1)S(1)}, u32[]{:S(2)}, u32[]{:S(2)}) collective-permute-start(bf16[1,128,2048]{2,1,0:T(8,128)(2,1)S(1)} %get-tuple-element.132), channel_id=1, source_target_pairs={{4,0},{5,1},{6,2},{7,3},{8,4},{9,5},{10,6},{11,7},{12,8},{13,9},{1... | collective-permute-start | bytes 1572872 | tf_op jit(solution)/shard_map/ppermute | solution.py:16
  390.0 30.3 %collective-permute-start.16 = (bf16[1,128,2048]{2,1,0:T(8,128)(2,1)S(1)}, bf16[1,128,2048]{2,1,0:T(8,128)(2,1)S(1)}, u32[]{:S(2)}, u32[]{:S(2)}) collective-permute-start(bf16[1,128,2048]{2,1,0:T(8,128)(2,1)S(1)} %get-tuple-element.132), channel_id=1, source_target_pairs={{5,0},{6,1},{7,2},{8,3},{9,4},{10,5},{11,6},{12,7},{13,8},{14,9},{... | collective-permute-start | bytes 1572872 | tf_op jit(solution)/shard_map/ppermute | solution.py:16
  421.2 58.7 %copy-start.5 = (bf16[128,1024]{1,0:T(8,128)(2,1)S(1)}, bf16[128,1024]{1,0:T(8,128)(2,1)}, u32[]{:S(2)}) copy-start(bf16[128,1024]{1,0:T(8,128)(2,1)} %copy-done.4) | copy-start | bytes 786436
  (4 other events, 20.8 us)
Sparse Core Ops, SparseCore 0:
  10.1 157.5 all-gather.2
  170.5 111.0 all-gather.4
where the time goes:
time: 491 us; the launch traced here: 488 us
  waiting for transfers between devices  341 us (69%)
  starting transfers between devices  45.6 us (9%)
  local copies, waits for them, and re-layouts  45.5 us (9%)
  matrix products  26.8 us (5%)
  other arithmetic  14.5 us (3%)
  between operations  13.7 us (3%)
    ppermute x17, waiting for transfers between devices, from_behind(): return lax.ppermute(block, axis, route)  158 us
    all_gather x1, waiting for transfers between devices, local(): lax.all_gather(w_down, 'seq', axis=1, tiled=True)  114 us
    all_gather x1, waiting for transfers between devices, local(): lax.all_gather(w_up, 'seq', axis=1, tiled=True)  67.6 us
    ppermute x17, starting transfers between devices, from_behind(): return lax.ppermute(block, axis, route)  45.6 us
    unnamed x30, local copies, waits for them, and re-layouts  19.1 us
    another operation x6, local copies, waits for them, and re-layouts  12.3 us
    dot_general x1, matrix products, finish(): jnp.dot(hidden, down_weight, preferred_element_type=jnp.float32)  10 us
  transfers between devices with their start and end apart: 19, of which 13 were waited for; matrix products, arithmetic and copies ran while one was open for 4% of the time, Pallas kernels for 0%

commit v1 on v0

v1 whole, which is shorter than its diff:
```python
import functools
import math

import jax
import jax.numpy as jnp
from jax import lax
from jax.experimental import pallas as pl
from jax.experimental.pallas import tpu as pltpu
from jax.sharding import PartitionSpec as P

HEADS = 16
BLK = 128
ROW = 4
GROUP = 4
TILE = 256
MESH = pl.DeviceIdType.MESH
NT = (((1,), (1,)), ((), ()))


def normalise(widened, gain):
    mean = jnp.mean(widened * widened, axis=-1, keepdims=True)
    return (widened * lax.rsqrt(mean + 1e-05) * gain).astype(jnp.bfloat16)


def kernel(
    n, ids, count, tokens, w_query, w_key, w_value, w_out, gain, w_up, w_down, second_gain,
    out,
    around, normed, queries, keys, values, mixed, attended, second, hidden, total, leaving,
    landing, finished, wq, wk, wv, wo, up, down,
    local_sem, x_send, x_recv, o_send, w_send, w_recv, s_send, s_recv, p_send, p_recv, go,
):
    section, seq = lax.axis_index("section"), lax.axis_index("seq")
    row, col = lax.div(seq, ROW), lax.rem(seq, ROW)
    rows = n // ROW
    width = wq.shape[0]
    units = w_up.shape[1]
    mine = lax.rem(row, GROUP)
    members = n // GROUP
    member = lax.div(row, GROUP) * ROW + col
    pairs = HEADS // 2
    tiles = width // TILE

    def local(src, dst, index):
        return pltpu.make_async_copy(src, dst, local_sem.at[index])

    own_up = pl.ds(pl.multiple_of(member * units, units), units)
    locals_ = [
        local(w_query.at[0], wq, 0),
        local(w_key.at[0], wk, 1),
        local(w_value.at[0], wv, 2),
        local(w_out.at[0], wo, 3),
        local(w_up.at[0], up.at[own_up], 4),
        local(w_down.at[0], down.at[own_up], 5),
    ]
    own_tokens = local(tokens.at[0], around.at[4], 6)

    @pl.when(section == 0)
    def _():
        own_tokens.start()

    for copy in locals_:
        copy.start()

    barrier = pltpu.get_barrier_semaphore()

    def greet(step, carry):
        other = lax.rem(section * n + seq + 1 + step, 2 * n)
        pl.semaphore_signal(barrier, inc=1, device_id=(lax.div(other, n), lax.rem(other, n)), device_id_type=MESH)
        return carry

    lax.fori_loop(0, 2 * n - 1, greet, 0)
    pl.semaphore_wait(barrier, 2 * n - 1)

    def beside(slot):
        dr, dc = slot // 3 - 1, slot % 3 - 1
        exists = (row + dr >= 0) & (row + dr < rows) & (col + dc >= 0) & (col + dc < ROW)
        return exists, jnp.clip(row + dr, 0, rows - 1) * ROW + jnp.clip(col + dc, 0, ROW - 1)

    def token_copy(slot):
        device = beside(slot)[1]
        return pltpu.make_async_remote_copy(
            tokens.at[0], around.at[8 - slot], x_send.at[slot], x_recv.at[8 - slot],
            device_id=(section, device), device_id_type=MESH)

    def result_copy(slot):
        device = beside(slot)[1]
        return pltpu.make_async_remote_copy(
            finished, around.at[8 - slot], o_send.at[slot], x_recv.at[8 - slot],
            device_id=(1, device), device_id_type=MESH)

    def arrival(slot):
        return pltpu.make_async_remote_copy(
            finished, around.at[slot], o_send.at[slot], x_recv.at[slot],
            device_id=(section, seq), device_id_type=MESH)

    def weight_copies(step, which):
        place = lax.rem(member + step, members)
        device = (lax.div(place, ROW) * GROUP + mine) * ROW + lax.rem(place, ROW)
        src, dst = (w_up, up) if which == 0 else (w_down, down)
        return pltpu.make_async_remote_copy(
            src.at[0], dst.at[own_up], w_send.at[2 * step + which], w_recv.at[2 * step + which],
            device_id=(section, device), device_id_type=MESH)

    def weight_arrival(step, which):
        place = lax.rem(member + members - step, members)
        there = pl.ds(pl.multiple_of(place * units, units), units)
        src, dst = (w_up, up) if which == 0 else (w_down, down)
        return pltpu.make_async_remote_copy(
            src.at[0], dst.at[there], w_send.at[2 * step + which], w_recv.at[2 * step + which],
            device_id=(section, seq), device_id_type=MESH)

    def each(body):
        if members > 8:
            lax.fori_loop(1, members, body, 0)
        else:
            for step in range(1, members):
                body(step, 0)

    @pl.when(section == 0)
    def _():
        for slot in (0, 2, 6, 8, 1, 7, 3, 5):
            @pl.when(beside(slot)[0])
            def _():
                token_copy(slot).start()

    @pl.when(section == 1)
    def _():
        pl.semaphore_wait(go, 1)

    def send_weights(step, carry):
        weight_copies(step, 0).start()
        weight_copies(step, 1).start()
        return carry

    each(send_weights)

    def await_slot(slot):
        exists = beside(slot)[0]

        @pl.when(exists)
        def _():
            arrival(slot).wait_recv()

        @pl.when(jnp.logical_not(exists))
        def _():
            around[slot] = jnp.zeros((BLK, width), jnp.bfloat16)

    @pl.when(section == 0)
    def _():
        own_tokens.wait()

    @pl.when(section == 1)
    def _():
        arrival(4).wait_recv()

    entries = ids[...]
    listed = lax.broadcasted_iota(jnp.int32, entries.shape, 1) < count[...]
    flags = []
    for slot in range(9):
        exists, device = beside(slot)
        wanted = jnp.where(exists, device, jnp.int32(-1))
        hit = jnp.where(listed & (entries == wanted), 1.0, 0.0)
        flags.append(jnp.broadcast_to(jnp.max(hit, axis=1, keepdims=True), (1, BLK)))
    live_row = jnp.concatenate(flags, axis=1)

    gain_row = gain[...]
    normed[pl.ds(0, BLK)] = normalise(around[4].astype(jnp.float32), gain_row)
    locals_[0].wait()

    score_scale = 1.0 / math.sqrt(width // HEADS)

    def query_tile(step, carry):
        at = pl.ds(pl.multiple_of(step * TILE, TILE), TILE)
        product = jnp.dot(normed[pl.ds(0, BLK)], wq[:, at], preferred_element_type=jnp.float32)
        queries[:, at] = (product.astype(jnp.bfloat16).astype(jnp.float32) * score_scale).astype(jnp.bfloat16)
        return carry

    lax.fori_loop(0, tiles, query_tile, 0)
    locals_[1].wait()
    locals_[2].wait()

    for part in (1, 0, 2):
        for slot in range(3 * part, 3 * part + 3):
            if slot != 4:
                await_slot(slot)
        for slot in range(3):
            normed[pl.ds(slot * BLK, BLK)] = normalise(
                around[3 * part + slot].astype(jnp.float32), gain_row)

        def key_tile(step, carry):
            at = pl.ds(pl.multiple_of(step * TILE, TILE), TILE)
            there = pl.ds(3 * part * BLK, 3 * BLK)
            keys[there, at] = jnp.dot(
                normed[...], wk[:, at], preferred_element_type=jnp.float32).astype(jnp.bfloat16)
            values[there, at] = jnp.dot(
                normed[...], wv[:, at], preferred_element_type=jnp.float32).astype(jnp.bfloat16)
            return carry

        lax.fori_loop(0, tiles, key_tile, 0)

    first_half = lax.broadcasted_iota(jnp.int32, (BLK, 128), 1) < 64

    def head_pair(pair, carry):
        at = pl.ds(pl.multiple_of(pair * 128, 128), 128)
        q = queries[:, at]
        zero = jnp.zeros_like(q)
        both = jnp.concatenate([jnp.where(first_half, q, zero), jnp.where(first_half, zero, q)], axis=0)
        scores = lax.dot_general(both, keys[:, at], NT, preferred_element_type=jnp.float32)
        scores = jnp.where(live_row > 0.0, scores, -jnp.inf)
        exponent = jnp.exp(scores - jnp.max(scores, axis=-1, keepdims=True))
        divisor = jnp.sum(exponent, axis=-1, keepdims=True)
        product = jnp.dot(
            exponent.astype(jnp.bfloat16), values[:, at], preferred_element_type=jnp.float32) / divisor
        mixed[:, at] = jnp.where(first_half, product[:BLK], product[BLK:]).astype(jnp.bfloat16)
        return carry

    lax.fori_loop(0, pairs, head_pair, 0)
    locals_[3].wait()

    def out_tile(step, carry):
        at = pl.ds(pl.multiple_of(step * TILE, TILE), TILE)
        product = jnp.dot(mixed[...], wo[:, at], preferred_element_type=jnp.float32)
        attended[:, at] = (around[4, :, at].astype(jnp.float32) + product).astype(jnp.bfloat16)
        return carry

    lax.fori_loop(0, tiles, out_tile, 0)
    second[mine] = normalise(attended[...].astype(jnp.float32), second_gain[...])

    def peer(step):
        return lax.rem(mine + step, GROUP)

    def peer_device(step):
        return (lax.div(row, GROUP) * GROUP + peer(step)) * ROW + col

    def second_copy(step):
        return pltpu.make_async_remote_copy(
            second.at[mine], second.at[mine], s_send.at[step], s_recv.at[step],
            device_id=(section, peer_device(step)), device_id_type=MESH)

    def second_arrival(step):
        return pltpu.make_async_remote_copy(
            second.at[mine], second.at[peer(step)], s_send.at[step], s_recv.at[GROUP - step],
            device_id=(section, peer_device(step)), device_id_type=MESH)

    def partial_copy(step):
        return pltpu.make_async_remote_copy(
            leaving.at[step], landing.at[step], p_send.at[step], p_recv.at[step],
            device_id=(section, peer_device(step)), device_id_type=MESH)

    for step in range(1, GROUP):
        second_copy(step).start()

    locals_[4].wait()
    locals_[5].wait()

    def await_weights(step, carry):
        weight_arrival(step, 0).wait_recv()
        weight_arrival(step, 1).wait_recv()
        return carry

    each(await_weights)

    @pl.when(section == 0)
    def _():
        pl.semaphore_signal(go, inc=1, device_id=(1, seq), device_id_type=MESH)

    for step in range(GROUP):
        if step:
            second_arrival(step).wait_recv()
        rows_in = second.at[peer(step)]

        def up_tile(tile, carry):
            at = pl.ds(pl.multiple_of(tile * TILE, TILE), TILE)
            raised = lax.dot_general(rows_in[...], up[at], NT, preferred_element_type=jnp.float32)
            hidden[:, at] = jax.nn.gelu(raised, approximate=True).astype(jnp.bfloat16)
            return carry

        lax.fori_loop(0, up.shape[0] // TILE, up_tile, 0)

        def down_tile(tile, carry):
            at = pl.ds(pl.multiple_of(tile * TILE, TILE), TILE)
            product = jnp.dot(hidden[...], down[:, at], preferred_element_type=jnp.float32)
            if step:
                leaving[step, :, at] = product.astype(jnp.bfloat16)
            else:
                total[:, at] = product
            return carry

        lax.fori_loop(0, tiles, down_tile, 0)
        if step:
            partial_copy(step).start()

    gathered = attended[...].astype(jnp.float32) + total[...]
    for step in range(1, GROUP):
        partial_copy(step).wait_recv()
        gathered = gathered + landing[step].astype(jnp.float32)
    result = gathered.astype(jnp.bfloat16)
    finished[...] = result
    out[0, 0] = result

    @pl.when(section == 0)
    def _():
        for slot in (0, 2, 6, 8, 1, 7, 3, 5, 4):
            @pl.when(beside(slot)[0])
            def _():
                result_copy(slot).start()
        for slot in range(9):
            @pl.when(beside(slot)[0])
            def _():
                result_copy(slot).wait_send()
                if slot != 4:
                    token_copy(slot).wait_send()

    for step in range(1, GROUP):
        second_copy(step).wait_send()
        partial_copy(step).wait_send()

    def drain(step, carry):
        weight_copies(step, 0).wait_send()
        weight_copies(step, 1).wait_send()
        return carry

    each(drain)


def solution(mesh):
    n = mesh.shape["seq"]

    def local(tokens, ids, count, w_query, w_key, w_value, w_out, gain, w_up, w_down, second_gain):
        width = tokens.shape[-1]
        held = w_up.shape[1] * n // GROUP
        members = n // GROUP
        bf16, f32 = jnp.bfloat16, jnp.float32
        any_ = pl.BlockSpec(memory_space=pl.ANY)
        vmem = pl.BlockSpec(memory_space=pltpu.VMEM)
        dma = pltpu.SemaphoreType.DMA
        return pl.pallas_call(
            functools.partial(kernel, n),
            out_shape=jax.ShapeDtypeStruct((1,) + tokens.shape, bf16),
            in_specs=[vmem, vmem, any_, any_, any_, any_, any_, vmem, any_, any_, vmem],
            out_specs=vmem,
            scratch_shapes=[
                pltpu.VMEM((9, BLK, width), bf16),
                pltpu.VMEM((3 * BLK, width), bf16),
                pltpu.VMEM((BLK, width), bf16),
                pltpu.VMEM((9 * BLK, width), bf16),
                pltpu.VMEM((9 * BLK, width), bf16),
                pltpu.VMEM((BLK, width), bf16),
                pltpu.VMEM((BLK, width), bf16),
                pltpu.VMEM((GROUP, BLK, width), bf16),
                pltpu.VMEM((BLK, held), bf16),
                pltpu.VMEM((BLK, width), f32),
                pltpu.VMEM((GROUP, BLK, width), bf16),
                pltpu.VMEM((GROUP, BLK, width), bf16),
                pltpu.VMEM((BLK, width), bf16),
                pltpu.VMEM((width, width), bf16),
                pltpu.VMEM((width, width), bf16),
                pltpu.VMEM((width, width), bf16),
                pltpu.VMEM((width, width), bf16),
                pltpu.VMEM((held, width), bf16),
                pltpu.VMEM((held, width), bf16),
                dma((7,)),
                dma((9,)),
                dma((9,)),
                dma((9,)),
                dma((2 * members,)),
                dma((2 * members,)),
                dma((GROUP,)),
                dma((GROUP,)),
                dma((GROUP,)),
                dma((GROUP,)),
                pltpu.SemaphoreType.REGULAR,
            ],
            compiler_params=pltpu.CompilerParams(
                collective_id=0, has_side_effects=True, vmem_limit_bytes=48 * 1024 * 1024),
        )(ids, count.reshape(1, 1), tokens, w_query, w_key, w_value, w_out, gain, w_up, w_down, second_gain)

    in_specs = (
        P(None, "seq", None),
        P("seq", None),
        P("seq"),
        P("section", None, None),
        P("section", None, None),
        P("section", None, None),
        P("section", None, None),
        P("section", None),
        P("section", "seq", None),
        P("section", "seq", None),
        P("section", None),
    )
    return jax.shard_map(
        local, mesh=mesh, in_specs=in_specs, out_specs=P("section", None, "seq", None), check_vma=False)
```

time: 491 us -> 138 us (0.28)
  waiting for transfers between devices: 341 us -> 0 us
  Pallas kernels: 0 us -> 127 us
  starting transfers between devices: 45.6 us -> 0 us
  local copies, waits for them, and re-layouts: 45.5 us -> 8.94 us
  matrix products: 26.8 us -> 0 us
  other arithmetic: 14.5 us -> 0 us
  between operations: 13.7 us -> 0.68 us
    all_gather x2 -> x0, waiting for transfers between devices: 181 us -> none  [the longest x1 114 us: local(): lax.all_gather(w_down, 'seq', axis=1, tiled=True)]
    ppermute x17 -> x0, waiting for transfers between devices: 158 us -> none  [from_behind(): return lax.ppermute(block, axis, route)]
    pallas_call x0 -> x1, Pallas kernels: none -> 127 us  [local(): pl.pallas_call(functools.partial(kernel, n), out_shape=jax.ShapeDtypeStru...]
    ppermute x17 -> x0, starting transfers between devices: 45.6 us -> none  [from_behind(): return lax.ppermute(block, axis, route)]
    dot_general x7 -> x0, matrix products: 26.8 us -> none  [the longest x1 10 us: finish(): jnp.dot(hidden, down_weight, preferred_element_type=jnp.float32)]
    another operation x6 -> x0, local copies, waits for them, and re-layouts: 12.3 us -> none
    unnamed x30 -> x17, local copies, waits for them, and re-layouts: 19.1 us -> 8.94 us
    sub x1 -> x0, other arithmetic: 6.68 us -> none  [soft_weights(): exponent = jnp.exp(scaled - row_max)]
  transfers between devices with their start and end apart: 19 -> 0, of which waited for: 13 -> 0; matrix products, arithmetic and copies ran while one was open for 4% -> 0% of each run, Pallas kernels for 0% -> 0%
where the time goes in v1:
time: 138 us; the launch traced here: 137 us
  Pallas kernels  127 us (92%)
  local copies, waits for them, and re-layouts  8.94 us (6%)
    pallas_call x1, Pallas kernels, local(): pl.pallas_call(functools.partial(kernel, n), out_shape=jax.ShapeDtypeStru...  127 us
    unnamed x17, local copies, waits for them, and re-layouts  8.94 us

profile of v1, /device:TPU:13, one launch (start us, length us, event | category | flops | bytes accessed | tf_op | source)
XLA Modules:
  0.0 136.6 jit_solution(5942102621803531670)
XLA Ops:
  0.7 0.0 copy-start
  0.7 1.6 %copy-done = bf16[1,1024,1024]{2,1,0:T(8,128)(2,1)S(1)} copy-done((bf16[1,1024,1024]{2,1,0:T(8,128)(2,1)S(1)}, bf16[1,1024,1024]{2,1,0:T(8,128)(2,1)}, u32[]{:S(2)}) %copy-start) | copy-done | bytes 2097176
  2.2 0.0 copy-start.1
  2.2 1.6 %copy-done.1 = bf16[1,1024,1024]{2,1,0:T(8,128)(2,1)S(1)} copy-done((bf16[1,1024,1024]{2,1,0:T(8,128)(2,1)S(1)}, bf16[1,1024,1024]{2,1,0:T(8,128)(2,1)}, u32[]{:S(2)}) %copy-start.1) | copy-done | bytes 2097176
  3.8 0.0 copy-start.2
  3.8 1.0 copy-done.2
  4.9 0.0 copy-start.3
  4.9 1.0 copy-done.3
  5.9 0.0 copy-start.4
  5.9 0.9 copy-done.4
  6.9 0.0 copy-start.5
  6.9 0.7 copy-done.5
  7.6 0.0 copy-start.6
  7.6 0.7 copy-done.6
  8.2 0.0 copy-start.7
  8.2 0.7 copy-done.7
  8.9 127.0 %shard_map.109 = bf16[1,1,128,1024]{3,2,1,0:T(8,128)(2,1)S(1)} custom-call(s32[1,9]{1,0:T(1,128)S(1)} %copy-done.7, s32[1,1]{1,0:T(1,128)} %bitcast.1.count, bf16[1,128,1024]{2,1,0:T(8,128)(2,1)S(1)} %copy-done.4, bf16[1,1024,1024]{2,1,0:T(8,128)(2,1)S(1)} %copy-done, bf16[1,1024,1024]{2,1,0:T(8,128)(2,1)S(1)} %copy-done.1, bf16[1,1024,1024]{2,1,0:T(8,128)(2,1)} %w_value.1, ...), custom_call_target="tpu_custom_call" | custom-call | tf_op jit(solution)/shard_map/pallas_call | solution.py:337
  135.9 0.7 copy.14
Async XLA Ops:
  0.7 1.6 %copy-start = (bf16[1,1024,1024]{2,1,0:T(8,128)(2,1)S(1)}, bf16[1,1024,1024]{2,1,0:T(8,128)(2,1)}, u32[]{:S(2)}) copy-start(bf16[1,1024,1024]{2,1,0:T(8,128)(2,1)} %w_query.1) | copy-start | bytes 6291460
  2.2 1.6 %copy-start.1 = (bf16[1,1024,1024]{2,1,0:T(8,128)(2,1)S(1)}, bf16[1,1024,1024]{2,1,0:T(8,128)(2,1)}, u32[]{:S(2)}) copy-start(bf16[1,1024,1024]{2,1,0:T(8,128)(2,1)} %w_key.1) | copy-start | bytes 6291460
  3.8 1.0 copy-start.2
  4.9 1.0 copy-start.3
  5.9 0.9 copy-start.4
  6.9 0.7 copy-start.5
  7.6 0.7 copy-start.6
  8.2 0.7 copy-start.7

commit v2 on v1

--- a/solution.py
+++ b/solution.py
@@ -27,7 +27,7 @@
     out,
     around, normed, queries, keys, values, mixed, attended, second, hidden, total, leaving,
     landing, finished, wq, wk, wv, wo, up, down,
-    local_sem, x_send, x_recv, o_send, w_send, w_recv, s_send, s_recv, p_send, p_recv, go,
+    local_sem, x_send, x_recv, o_send, w_send, w_recv, s_send, s_recv, p_send, p_recv, go, f_send,
 ):
     section, seq = lax.axis_index("section"), lax.axis_index("seq")
     row, col = lax.div(seq, ROW), lax.rem(seq, ROW)
@@ -79,7 +79,7 @@
     def token_copy(slot):
         device = beside(slot)[1]
         return pltpu.make_async_remote_copy(
-            tokens.at[0], around.at[8 - slot], x_send.at[slot], x_recv.at[8 - slot],
+            around.at[4], around.at[8 - slot], x_send.at[slot], x_recv.at[8 - slot],
             device_id=(section, device), device_id_type=MESH)
 
     def result_copy(slot):
@@ -87,6 +87,15 @@
         return pltpu.make_async_remote_copy(
             finished, around.at[8 - slot], o_send.at[slot], x_recv.at[8 - slot],
             device_id=(1, device), device_id_type=MESH)
+
+    def relay(index):
+        side, up_or_down = index % 2 * 2, index // 2 * 2
+        device = beside(3 * up_or_down + 1)[1]
+        slot = 3 * (2 - up_or_down) + side
+        exists = beside(3 + side)[0] & beside(3 * up_or_down + 1)[0]
+        return exists, pltpu.make_async_remote_copy(
+            around.at[3 + side], around.at[slot], f_send.at[index], x_recv.at[slot],
+            device_id=(section, device), device_id_type=MESH)
 
     def arrival(slot):
         return pltpu.make_async_remote_copy(
@@ -118,7 +127,8 @@
 
     @pl.when(section == 0)
     def _():
-        for slot in (0, 2, 6, 8, 1, 7, 3, 5):
+        own_tokens.wait()
+        for slot in (3, 5, 1, 7):
             @pl.when(beside(slot)[0])
             def _():
                 token_copy(slot).start()
@@ -144,10 +154,6 @@
         @pl.when(jnp.logical_not(exists))
         def _():
             around[slot] = jnp.zeros((BLK, width), jnp.bfloat16)
-
-    @pl.when(section == 0)
-    def _():
-        own_tokens.wait()
 
     @pl.when(section == 1)
     def _():
@@ -183,6 +189,11 @@
         for slot in range(3 * part, 3 * part + 3):
             if slot != 4:
                 await_slot(slot)
+            for index in range(4):
+                if slot == 3 + index % 2 * 2:
+                    @pl.when(relay(index)[0])
+                    def _():
+                        relay(index)[1].start()
         for slot in range(3):
             normed[pl.ds(slot * BLK, BLK)] = normalise(
                 around[3 * part + slot].astype(jnp.float32), gain_row)
@@ -300,17 +311,22 @@
 
     @pl.when(section == 0)
     def _():
-        for slot in (0, 2, 6, 8, 1, 7, 3, 5, 4):
+        for slot in (4, 3, 5, 1, 7):
             @pl.when(beside(slot)[0])
             def _():
                 result_copy(slot).start()
-        for slot in range(9):
+        for slot in (4, 3, 5, 1, 7):
             @pl.when(beside(slot)[0])
             def _():
                 result_copy(slot).wait_send()
                 if slot != 4:
                     token_copy(slot).wait_send()
 
+    for index in range(4):
+        @pl.when(relay(index)[0])
+        def _():
+            relay(index)[1].wait_send()
+
     for step in range(1, GROUP):
         second_copy(step).wait_send()
         partial_copy(step).wait_send()
@@ -331,7 +347,7 @@
         held = w_up.shape[1] * n // GROUP
         members = n // GROUP
         bf16, f32 = jnp.bfloat16, jnp.float32
-        any_ = pl.BlockSpec(memory_space=pl.ANY)
+        any_ = pl.BlockSpec(memory_space=pltpu.HBM)
         vmem = pl.BlockSpec(memory_space=pltpu.VMEM)
         dma = pltpu.SemaphoreType.DMA
         return pl.pallas_call(
@@ -370,9 +386,10 @@
                 dma((GROUP,)),
                 dma((GROUP,)),
                 pltpu.SemaphoreType.REGULAR,
+                dma((4,)),
             ],
             compiler_params=pltpu.CompilerParams(
-                collective_id=0, has_side_effects=True, vmem_limit_bytes=48 * 1024 * 1024),
+                collective_id=0, has_side_effects=True, vmem_limit_bytes=56 * 1024 * 1024),
         )(ids, count.reshape(1, 1), tokens, w_query, w_key, w_value, w_out, gain, w_up, w_down, second_gain)
 
     in_specs = (

time: 138 us -> 117 us (0.85)
  Pallas kernels: 127 us -> 114 us
  local copies, waits for them, and re-layouts: 8.94 us -> 1.67 us
    pallas_call x1, Pallas kernels: 127 us -> 114 us  [local(): pl.pallas_call(functools.partial(kernel, n), out_shape=jax.ShapeDtypeStru...]
    unnamed x17 -> x1, local copies, waits for them, and re-layouts: 8.94 us -> 1.67 us
where the time goes in v2:
time: 117 us; the launch traced here: 116 us
  Pallas kernels  114 us (97%)
  local copies, waits for them, and re-layouts  1.67 us (1%)
    pallas_call x1, Pallas kernels, local(): pl.pallas_call(functools.partial(kernel, n), out_shape=jax.ShapeDtypeStru...  114 us

profile of v2, /device:TPU:13, one launch (start us, length us, event | category | flops | bytes accessed | tf_op | source)
XLA Modules:
  0.0 116.4 jit_solution(9043776562812111148)
XLA Ops:
  0.7 114.1 %shard_map.109 = bf16[1,1,128,1024]{3,2,1,0:T(8,128)(2,1)} custom-call(s32[1,9]{1,0:T(1,128)} %ids.1, s32[1,1]{1,0:T(1,128)} %bitcast.1.count, bf16[1,128,1024]{2,1,0:T(8,128)(2,1)} %tokens.1, bf16[1,1024,1024]{2,1,0:T(8,128)(2,1)} %w_query.1, bf16[1,1024,1024]{2,1,0:T(8,128)(2,1)} %w_key.1, bf16[1,1024,1024]{2,1,0:T(8,128)(2,1)} %w_value.1, ...), custom_call_target="tpu_custom_call" | custom-call | tf_op jit(solution)/shard_map/pallas_call | solution.py:353
  114.7 1.7 %copy.14 = bf16[1,1,128,1024]{3,2,1,0:T(8,128)(2,1)} copy(bf16[1,1,128,1024]{3,2,1,0:T(8,128)(2,1)} %shard_map.109) | data formatting | bytes 524288

commit v3 on v2

--- a/solution.py
+++ b/solution.py
@@ -238,7 +238,9 @@
     second[mine] = normalise(attended[...].astype(jnp.float32), second_gain[...])
 
     def peer(step):
-        return lax.rem(mine + step, GROUP)
+        if step == 1:
+            return mine + 1 - 2 * lax.rem(mine, 2)
+        return mine if step == 0 else lax.rem(mine + 2, GROUP) if step == 2 else GROUP - 1 - mine
 
     def peer_device(step):
         return (lax.div(row, GROUP) * GROUP + peer(step)) * ROW + col
@@ -250,7 +252,7 @@
 
     def second_arrival(step):
         return pltpu.make_async_remote_copy(
-            second.at[mine], second.at[peer(step)], s_send.at[step], s_recv.at[GROUP - step],
+            second.at[mine], second.at[peer(step)], s_send.at[step], s_recv.at[step],
             device_id=(section, peer_device(step)), device_id_type=MESH)
 
     def partial_copy(step):

time: 117 us -> 116 us (level)
  no operation moved by 1% of the time
where the time goes in v3:
time: 116 us; the launch traced here: 115 us
  Pallas kernels  113 us (97%)
  local copies, waits for them, and re-layouts  1.67 us (1%)
    pallas_call x1, Pallas kernels, local(): pl.pallas_call(functools.partial(kernel, n), out_shape=jax.ShapeDtypeStru...  113 us

profile of v3, /device:TPU:13, one launch (start us, length us, event | category | flops | bytes accessed | tf_op | source)
XLA Modules:
  0.0 115.4 jit_solution(7017061029856493820)
XLA Ops:
  0.7 113.0 %shard_map.109 = bf16[1,1,128,1024]{3,2,1,0:T(8,128)(2,1)} custom-call(s32[1,9]{1,0:T(1,128)} %ids.1, s32[1,1]{1,0:T(1,128)} %bitcast.1.count, bf16[1,128,1024]{2,1,0:T(8,128)(2,1)} %tokens.1, bf16[1,1024,1024]{2,1,0:T(8,128)(2,1)} %w_query.1, bf16[1,1024,1024]{2,1,0:T(8,128)(2,1)} %w_key.1, bf16[1,1024,1024]{2,1,0:T(8,128)(2,1)} %w_value.1, ...), custom_call_target="tpu_custom_call" | custom-call | tf_op jit(solution)/shard_map/pallas_call | solution.py:355
  113.7 1.7 %copy.14 = bf16[1,1,128,1024]{3,2,1,0:T(8,128)(2,1)} copy(bf16[1,1,128,1024]{3,2,1,0:T(8,128)(2,1)} %shard_map.109) | data formatting | bytes 524288
